TPU v7x, 32 devices: a whole 2x2x4 slice. The times are simulated.
32 devices in a mesh: freq: 2 (over x), tile: 16 (over z, y, core).
Axes of the slice: x: 2, y: 2, z: 4, core: 2. Of those that a mesh axis runs over, the one named last changes fastest.
Arguments:
- data: float32 [4, 2048, 256], P('freq', 'tile'), parts along dimension 0, may hold values from -6 to 6
- x_init: float32 [4, 8192, 256], P('freq', 'tile'), parts along dimension 0, may hold values from -6 to 6
- ufac: bfloat16 [4, 2048, 256], P('freq', 'tile'), parts along dimension 0, may hold values from -0.1875 to 0.1875
- vfac: bfloat16 [4, 4, 16, 8192], P('freq', None, None, 'tile'), parts along dimension 0, may hold values from -0.25 to 0.25
Outputs:
- solution: float32 [4, 8192, 256], P('freq', 'tile'), parts along dimension 0
- residual: float32 [4, 2048, 256], P('freq', 'tile'), parts along dimension 0
There are 2 independent parts, one for each index of `freq`. A program takes and returns all parts, laid end to end along the dimension named above; each array names one. Nothing has to cross between parts.
All inputs are finite; a program needn't handle non-finite values.
Results may differ from a plain program's by a relative error of at most 0.0058.
Values may be sent and summed in bfloat16 or wider, within the bound.
No kernel may reach another device: no remote copies, remote signals or barrier semaphores. Data moves between devices by JAX's collectives and lax.ppermute only.
A program may use at most 64 MiB of HBM per device.

v0:
```python
import jax
import jax.numpy as jnp
from jax import lax
from jax.sharding import PartitionSpec as P

QV = 4
ITERS = 2
step_size = 0.4
threshold = 0.4


def complex_product(pattern, factors, vectors, conjugate):

    def single(factor_part, vector_part):
        return jnp.einsum(pattern, factor_part, vector_part, preferred_element_type=jnp.float32)

    if conjugate:
        real_part = single(factors[0], vectors[0]) + single(factors[1], vectors[1])
        imag_part = single(factors[0], vectors[1]) - single(factors[1], vectors[0])
    else:
        real_part = single(factors[0], vectors[0]) - single(factors[1], vectors[1])
        imag_part = single(factors[0], vectors[1]) + single(factors[1], vectors[0])
    return jnp.stack([real_part, imag_part])


def shrink(values):
    magnitude = jnp.sqrt(values[0] * values[0] + values[1] * values[1])
    shrink_factor = jnp.maximum(magnitude - threshold, 0.0) / jnp.maximum(magnitude, threshold)
    return values * shrink_factor


def body(data, x_init, ufac, vfac):
    tile_count = lax.axis_size("tile")
    tile_rows = vfac.shape[1]
    rank_width = vfac.shape[2]
    point_count = x_init.shape[2]
    estimate = x_init
    misfit = data
    for iteration in range(ITERS):
        xlow = estimate.astype(jnp.bfloat16)
        coeffs = complex_product("irk,kv->irv", vfac, xlow, True).astype(jnp.bfloat16)
        repeated = jnp.repeat(coeffs, QV, axis=1)
        received = lax.all_to_all(repeated, "tile", split_axis=1, concat_axis=1, tiled=True)
        flat_coeffs = received.reshape(2, tile_count * rank_width, point_count)
        predicted = complex_product("tk,kv->tv", ufac, flat_coeffs, False)
        misfit = data - predicted
        misfit_low = misfit.astype(jnp.bfloat16)
        partial_value = complex_product("tk,tv->kv", ufac, misfit_low, True).reshape(
            2, tile_count, rank_width, point_count
        )
        gathered = lax.all_to_all(partial_value, "tile", split_axis=1, concat_axis=1, tiled=True)
        summed = (
            gathered.reshape(2, tile_rows, QV, rank_width, point_count)
            .sum(axis=2)
            .astype(jnp.bfloat16)
        )
        gradient = complex_product("irk,irv->kv", vfac, summed, False)
        estimate = shrink(estimate + step_size * gradient)
    return (estimate, misfit)


def solution(mesh):
    in_specs = (
        P("freq", "tile", None),
        P("freq", "tile", None),
        P("freq", "tile", None),
        P("freq", None, None, "tile"),
    )
    out_specs = (P("freq", "tile", None), P("freq", "tile", None))
    return jax.shard_map(body, mesh=mesh, in_specs=in_specs, out_specs=out_specs, check_vma=False)
```

profile of v0, /device:TPU:0, one launch (start us, length us, event | category | flops | bytes accessed | tf_op | source)
XLA Modules:
  0.0 85.4 jit_solution(18116899990691036280)
XLA Ops:
  0.6 0.0 copy-start.2
  0.6 1.3 %convert_element_type.20 = bf16[2,512,256]{2,1,0:T(8,128)(2,1)S(1)} convert(f32[2,512,256]{2,1,0:T(8,128)} %param.5) | non-fusion elementwise | flops 262144 | bytes 1572864 | tf_op jit(solution)/shard_map/convert_element_type | solution.py:40
  2.0 0.0 copy-done.2
  2.0 0.2 fusion.28
  2.1 0.2 fusion.27
  2.3 0.2 fusion.18
  2.5 0.2 fusion.19
  2.7 0.7 broadcast_in_dim.8
  3.4 0.0 copy-start.5
  3.4 7.5 %all-to-all-start = ((bf16[2,16,16,256]{3,2,0,1:T(8,128)(2,1)}), bf16[2,16,16,256]{3,2,0,1:T(8,128)(2,1)S(1)}, u32[]{:S(2)}, u32[]{:S(2)}) async-start(bf16[2,16,16,256]{3,2,0,1:T(8,128)(2,1)} %bitcast.8), calls=%async_computation | async-start | bytes 524288 | tf_op jit(solution)/shard_map/all_to_all | solution.py:43
  11.0 0.0 copy-done.5
  11.0 0.1 copy.31
  11.1 0.0 copy-start
  11.1 9.9 %all-to-all-done = bf16[2,16,16,256]{3,2,0,1:T(8,128)(2,1)S(1)} async-done(((bf16[2,16,16,256]{3,2,0,1:T(8,128)(2,1)}), bf16[2,16,16,256]{3,2,0,1:T(8,128)(2,1)S(1)}, u32[]{:S(2)}, u32[]{:S(2)}) %all-to-all-start) | async-done | bytes 262176 | tf_op jit(solution)/shard_map/all_to_all | solution.py:43
  21.0 0.0 copy-done
  21.0 0.2 fusion.51
  21.3 0.2 fusion.53
  21.5 0.2 fusion.10
  21.7 0.2 fusion.11
  22.0 0.2 fusion.47
  22.2 0.2 fusion.49
  22.4 0.2 convolution_subtract_fusion.1
  22.7 0.2 convolution_add_fusion.1
  22.9 0.0 copy-start.1
  22.9 0.8 pad_maximum_fusion
  23.8 3.6 %all-to-all-start.1 = ((f32[2,16,16,256]{3,2,0,1:T(8,128)}), f32[2,16,16,256]{3,2,0,1:T(8,128)S(1)}, u32[]{:S(2)}, u32[]{:S(2)}) async-start(f32[2,16,16,256]{3,2,0,1:T(8,128)} %pad_maximum_fusion), calls=%async_computation.1 | async-start | bytes 1048576 | tf_op jit(solution)/shard_map/all_to_all | solution.py:51
  27.3 0.0 copy-done.1
  27.3 0.3 copy.35
  27.7 13.9 %all-to-all-done.1 = f32[2,16,16,256]{3,2,0,1:T(8,128)S(1)} async-done(((f32[2,16,16,256]{3,2,0,1:T(8,128)}), f32[2,16,16,256]{3,2,0,1:T(8,128)S(1)}, u32[]{:S(2)}, u32[]{:S(2)}) %all-to-all-start.1) | async-done | bytes 524320 | tf_op jit(solution)/shard_map/all_to_all | solution.py:51
  41.6 0.2 convolution_bitcast_fusion.6
  41.9 0.2 convolution_bitcast_fusion.4
  42.1 0.3 fusion.1
  42.4 0.2 fusion.3
  42.6 0.2 fusion.20
  42.9 0.3 divide_bitcast_fusion.1
  43.1 0.3 multiply_convert_fusion
  43.5 0.2 fusion.30
  43.7 0.2 fusion.29
  43.9 0.2 fusion.16
  44.1 0.2 fusion.17
  44.3 13.9 %all_to_all.20 = bf16[2,16,16,256]{3,2,0,1:T(8,128)(2,1)S(1)} all-to-all(bf16[2,16,16,256]{3,2,0,1:T(8,128)(2,1)S(1)} %bitcast.250), channel_id=1, replica_groups=mesh['freq'=2,'tile'=16] {'tile'}, dimensions={1} | all-to-all | bytes 524288 | tf_op jit(solution)/shard_map/all_to_all | solution.py:43
  58.3 0.2 fusion.43
  58.5 0.2 fusion.45
  58.7 0.2 fusion.8
  58.9 0.2 fusion.9
  59.2 0.7 fusion.103
  59.9 0.2 fusion.39
  60.1 0.2 fusion.41
  60.4 0.2 convolution_subtract_fusion
  60.6 0.2 convolution_add_fusion
  60.8 0.8 pad_maximum_fusion.1
  61.7 3.7 %all-to-all-start.3 = ((f32[2,16,16,256]{3,2,0,1:T(8,128)}), f32[2,16,16,256]{3,2,0,1:T(8,128)S(1)}, u32[]{:S(2)}, u32[]{:S(2)}) async-start(f32[2,16,16,256]{3,2,0,1:T(8,128)} %pad_maximum_fusion.1), calls=%async_computation.3 | async-start | bytes 1048576 | tf_op jit(solution)/shard_map/all_to_all | solution.py:51
  65.4 0.0 copy-done.4
  65.4 0.8 copy.46
  66.2 13.4 %all-to-all-done.3 = f32[2,16,16,256]{3,2,0,1:T(8,128)S(1)} async-done(((f32[2,16,16,256]{3,2,0,1:T(8,128)}), f32[2,16,16,256]{3,2,0,1:T(8,128)S(1)}, u32[]{:S(2)}, u32[]{:S(2)}) %all-to-all-start.3) | async-done | bytes 524320 | tf_op jit(solution)/shard_map/all_to_all | solution.py:51
  79.7 0.0 copy-done.3
  79.7 0.2 convolution_bitcast_fusion.2
  79.9 0.2 convolution_bitcast_fusion
  80.2 0.3 fusion.5
  80.4 0.2 fusion.7
  80.7 0.4 fusion.21
  81.1 0.3 divide_bitcast_fusion
  81.4 1.5 %broadcast_multiply_fusion = f32[2,512,256]{1,2,0:T(8,128)} fusion(f32[512,256]{0,1:T(8,128)S(1)} %divide_bitcast_fusion, f32[1,512,256]{1,2,0:T(8,128)S(1)} %fusion.7, f32[1,512,256]{1,2,0:T(8,128)S(1)} %fusion.5, f32[512,256]{0,1:T(8,128)S(1)} %divide_bitcast_fusion.1, f32[2,512,256]{1,2,0:T(8,128)S(1)} %copy.35, f32[1,512,256]{1,2,0:T(8,128)S(1)} %fusion.3, ...), kind=kLoop, calls=%fused_computation.57 | loop fusion | flops 2097152 | bytes 5242880 | tf_op jit(solution)/shard_map/mul | solution.py:29
  82.9 2.5 %copy.45 = f32[2,512,256]{2,1,0:T(8,128)} copy(f32[2,512,256]{1,2,0:T(8,128)} %broadcast_multiply_fusion) | data formatting | bytes 2097152
  (12 shorter events, 0.2 us)
Async XLA Ops:
  0.6 1.3 %copy-start.2 = (bf16[2,4,16,512]{3,2,1,0:T(8,128)(2,1)S(1)}, bf16[2,4,16,512]{3,2,1,0:T(8,128)(2,1)}, u32[]{:S(2)}) copy-start(bf16[2,4,16,512]{3,2,1,0:T(8,128)(2,1)} %param.7) | copy-start | bytes 393220
  3.4 7.6 %copy-start.5 = (f32[2,128,256]{2,1,0:T(8,128)S(1)}, f32[2,128,256]{2,1,0:T(8,128)}, u32[]{:S(2)}) copy-start(f32[2,128,256]{2,1,0:T(8,128)} %param.4) | copy-start | bytes 786436
  3.4 17.6 %all-to-all-start = ((bf16[2,16,16,256]{3,2,0,1:T(8,128)(2,1)}), bf16[2,16,16,256]{3,2,0,1:T(8,128)(2,1)S(1)}, u32[]{:S(2)}, u32[]{:S(2)}) async-start(bf16[2,16,16,256]{3,2,0,1:T(8,128)(2,1)} %bitcast.8), calls=%async_computation | async-start | bytes 524288 | tf_op jit(solution)/shard_map/all_to_all | solution.py:43
  11.1 9.9 %copy-start = (bf16[2,128,256]{2,1,0:T(8,128)(2,1)S(1)}, bf16[2,128,256]{2,1,0:T(8,128)(2,1)}, u32[]{:S(2)}) copy-start(bf16[2,128,256]{2,1,0:T(8,128)(2,1)} %param.6) | copy-start | bytes 393220
  22.9 4.4 %copy-start.1 = (f32[2,512,256]{2,1,0:T(8,128)S(1)}, f32[2,512,256]{2,1,0:T(8,128)}, u32[]{:S(2)}) copy-start(f32[2,512,256]{2,1,0:T(8,128)} %param.5) | copy-start | bytes 3145732
  23.8 17.8 %all-to-all-start.1 = ((f32[2,16,16,256]{3,2,0,1:T(8,128)}), f32[2,16,16,256]{3,2,0,1:T(8,128)S(1)}, u32[]{:S(2)}, u32[]{:S(2)}) async-start(f32[2,16,16,256]{3,2,0,1:T(8,128)} %pad_maximum_fusion), calls=%async_computation.1 | async-start | bytes 1048576 | tf_op jit(solution)/shard_map/all_to_all | solution.py:51
  61.7 3.7 %copy-start.4 = (f32[2,128,256]{1,2,0:T(8,128)S(1)}, f32[2,128,256]{1,2,0:T(8,128)}, u32[]{:S(2)}) copy-start(f32[2,128,256]{1,2,0:T(8,128)} %get-tuple-element.9) | copy-start | bytes 786436
  61.7 17.9 %all-to-all-start.3 = ((f32[2,16,16,256]{3,2,0,1:T(8,128)}), f32[2,16,16,256]{3,2,0,1:T(8,128)S(1)}, u32[]{:S(2)}, u32[]{:S(2)}) async-start(f32[2,16,16,256]{3,2,0,1:T(8,128)} %pad_maximum_fusion.1), calls=%async_computation.3 | async-start | bytes 1048576 | tf_op jit(solution)/shard_map/all_to_all | solution.py:51
  66.2 13.4 %copy-start.3 = (bf16[2,4,16,512]{3,2,1,0:T(8,128)(2,1)S(1)}, bf16[2,4,16,512]{3,2,1,0:T(8,128)(2,1)}, u32[]{:S(2)}) copy-start(bf16[2,4,16,512]{3,2,1,0:T(8,128)(2,1)} %param.7) | copy-start | bytes 393220
where the time goes:
time: 85.9 us; the launch traced here: 85.4 us
  waiting for transfers between devices  37.1 us (43%)
  starting transfers between devices  14.8 us (17%)
  blocking collectives  13.9 us (16%)
  matrix products  7.03 us (8%)
  other arithmetic  6.81 us (8%)
  local copies, waits for them, and re-layouts  4.65 us (5%)
  between operations  1.04 us (1%)
    all_to_all x2, waiting for transfers between devices, body(): lax.all_to_all(partial_value, 'tile', split_axis=1, concat_axis=1, tiled=...  27.3 us
    all_to_all x1, blocking collectives, body(): lax.all_to_all(repeated, 'tile', split_axis=1, concat_axis=1, tiled=True)  13.9 us
    all_to_all x1, waiting for transfers between devices, body(): lax.all_to_all(repeated, 'tile', split_axis=1, concat_axis=1, tiled=True)  9.86 us
    all_to_all x1, starting transfers between devices, body(): lax.all_to_all(repeated, 'tile', split_axis=1, concat_axis=1, tiled=True)  7.55 us
    all_to_all x2, starting transfers between devices, body(): lax.all_to_all(partial_value, 'tile', split_axis=1, concat_axis=1, tiled=...  7.28 us
    dot_general x32, matrix products, single(): jnp.einsum(pattern, factor_part, vector_part, preferred_element_type=jnp....  7.03 us
    unnamed x16, local copies, waits for them, and re-layouts  3.85 us
    mul x3, other arithmetic, shrink(): return values * shrink_factor  1.99 us
  transfers between devices with their start and end apart: 3, of which 3 were waited for; matrix products, arithmetic and copies ran while one was open for 2% of the time, Pallas kernels for 0%

commit v1 on v0

--- a/solution.py
+++ b/solution.py
@@ -48,7 +48,12 @@
         partial_value = complex_product("tk,tv->kv", ufac, misfit_low, True).reshape(
             2, tile_count, rank_width, point_count
         )
-        gathered = lax.all_to_all(partial_value, "tile", split_axis=1, concat_axis=1, tiled=True)
+        gathered = jnp.concatenate(
+            lax.all_to_all(
+                jnp.stack(jnp.split(partial_value, lax.axis_size("tile"), axis=1)), "tile", 0, 0
+            ),
+            axis=1,
+        )
         summed = (
             gathered.reshape(2, tile_rows, QV, rank_width, point_count)
             .sum(axis=2)

time: 85.9 us -> 104 us (1.21)
  other arithmetic: 6.81 us -> 24.9 us
    unnamed x0 -> x30, other arithmetic: none -> 18.5 us
    another operation x4 -> x2, other arithmetic: 1.68 us -> 0.02 us  [complex_product(): return jnp.stack([real_part, imag_part])]
    another operation x0 -> x2, other arithmetic: none -> 1.23 us  [body(): jnp.stack(jnp.split(partial_value, lax.axis_size('tile'), axis=1))]
    unnamed x16 -> x12, local copies, waits for them, and re-layouts: 3.85 us -> 4.79 us
where the time goes in v1:
time: 104 us; the launch traced here: 103 us
  waiting for transfers between devices  36.2 us (35%)
  other arithmetic  24.9 us (24%)
  starting transfers between devices  14.7 us (14%)
  blocking collectives  13.9 us (13%)
  matrix products  7.01 us (7%)
  local copies, waits for them, and re-layouts  5.58 us (5%)
  between operations  1.04 us (1%)
    all_to_all x2, waiting for transfers between devices, body(): lax.all_to_all(jnp.stack(jnp.split(partial_value, lax.axis_size('tile'),...  26.3 us
    unnamed x30, other arithmetic  18.5 us
    all_to_all x1, blocking collectives, body(): lax.all_to_all(repeated, 'tile', split_axis=1, concat_axis=1, tiled=True)  13.9 us
    all_to_all x1, waiting for transfers between devices, body(): lax.all_to_all(repeated, 'tile', split_axis=1, concat_axis=1, tiled=True)  9.86 us
    all_to_all x1, starting transfers between devices, body(): lax.all_to_all(repeated, 'tile', split_axis=1, concat_axis=1, tiled=True)  7.55 us
    all_to_all x2, starting transfers between devices, body(): lax.all_to_all(jnp.stack(jnp.split(partial_value, lax.axis_size('tile'),...  7.15 us
    dot_general x32, matrix products, single(): jnp.einsum(pattern, factor_part, vector_part, preferred_element_type=jnp....  7.01 us
    unnamed x12, local copies, waits for them, and re-layouts  4.79 us
  transfers between devices with their start and end apart: 3, of which 3 were waited for; matrix products, arithmetic and copies ran while one was open for 2% of the time, Pallas kernels for 0%

profile of v1, /device:TPU:0, one launch (start us, length us, event | category | flops | bytes accessed | tf_op | source)
XLA Modules:
  0.0 103.3 jit_solution(4358416414586980024)
XLA Ops:
  0.6 1.3 %convert_element_type.20 = bf16[2,512,256]{2,1,0:T(8,128)(2,1)S(1)} convert(f32[2,512,256]{2,1,0:T(8,128)} %param.5) | non-fusion elementwise | flops 262144 | bytes 1572864 | tf_op jit(solution)/shard_map/convert_element_type | solution.py:40
  2.7 0.7 broadcast_in_dim.8
  3.4 7.5 %all-to-all-start = ((bf16[2,16,16,256]{3,2,0,1:T(8,128)(2,1)}), bf16[2,16,16,256]{3,2,0,1:T(8,128)(2,1)S(1)}, u32[]{:S(2)}, u32[]{:S(2)}) async-start(bf16[2,16,16,256]{3,2,0,1:T(8,128)(2,1)} %bitcast.8), calls=%async_computation | async-start | bytes 524288 | tf_op jit(solution)/shard_map/all_to_all | solution.py:43
  11.1 9.9 %all-to-all-done = bf16[2,16,16,256]{3,2,0,1:T(8,128)(2,1)S(1)} async-done(((bf16[2,16,16,256]{3,2,0,1:T(8,128)(2,1)}), bf16[2,16,16,256]{3,2,0,1:T(8,128)(2,1)S(1)}, u32[]{:S(2)}, u32[]{:S(2)}) %all-to-all-start) | async-done | bytes 262176 | tf_op jit(solution)/shard_map/all_to_all | solution.py:43
  21.5 0.2 fusion.10
  22.4 0.2 convolution_subtract_fusion.1
  22.7 0.2 convolution_add_fusion.1
  22.9 0.6 constant_dynamic-update-slice_fusion.15
  23.5 0.6 constant_dynamic-update-slice_fusion.14
  24.1 0.6 constant_dynamic-update-slice_fusion.13
  24.8 0.6 constant_dynamic-update-slice_fusion.12
  25.4 0.6 constant_dynamic-update-slice_fusion.11
  26.0 0.6 constant_dynamic-update-slice_fusion.10
  26.6 0.6 constant_dynamic-update-slice_fusion.9
  27.2 0.6 constant_dynamic-update-slice_fusion.8
  27.8 0.6 constant_dynamic-update-slice_fusion.7
  28.5 0.6 constant_dynamic-update-slice_fusion.6
  29.1 0.6 constant_dynamic-update-slice_fusion.5
  29.7 0.6 constant_dynamic-update-slice_fusion.4
  30.3 0.6 constant_dynamic-update-slice_fusion.3
  30.9 0.6 constant_dynamic-update-slice_fusion.2
  31.6 0.6 constant_dynamic-update-slice_fusion.1
  32.2 0.6 constant_dynamic-update-slice_fusion
  32.8 3.6 %all-to-all-start.1 = ((f32[16,2,1,16,256]{4,3,1,2,0:T(8,128)}), f32[16,2,1,16,256]{4,3,1,2,0:T(8,128)S(1)}, u32[]{:S(2)}, u32[]{:S(2)}) async-start(f32[16,2,1,16,256]{4,3,1,2,0:T(8,128)} %constant_dynamic-update-slice_fusion), calls=%async_computation.1 | async-start | bytes 1048576 | tf_op jit(solution)/shard_map/all_to_all | solution.py:52
  36.4 0.3 copy.63
  36.7 13.9 %all-to-all-done.1 = f32[16,2,1,16,256]{4,3,1,2,0:T(8,128)S(1)} async-done(((f32[16,2,1,16,256]{4,3,1,2,0:T(8,128)}), f32[16,2,1,16,256]{4,3,1,2,0:T(8,128)S(1)}, u32[]{:S(2)}, u32[]{:S(2)}) %all-to-all-start.1) | async-done | bytes 524320 | tf_op jit(solution)/shard_map/all_to_all | solution.py:52
  50.6 0.2 convolution_bitcast_fusion.6
  50.9 0.2 convolution_bitcast_fusion.4
  51.1 0.3 fusion.1
  51.4 0.2 fusion.3
  51.9 0.3 divide_bitcast_fusion.1
  52.2 0.3 multiply_convert_fusion
  53.4 13.9 %all_to_all.20 = bf16[2,16,16,256]{3,2,0,1:T(8,128)(2,1)S(1)} all-to-all(bf16[2,16,16,256]{3,2,0,1:T(8,128)(2,1)S(1)} %bitcast.438), channel_id=1, replica_groups=mesh['freq'=2,'tile'=16] {'tile'}, dimensions={1} | all-to-all | bytes 524288 | tf_op jit(solution)/shard_map/all_to_all | solution.py:43
  67.7 0.2 fusion.8
  68.2 0.7 fusion.135
  69.4 0.2 convolution_subtract_fusion
  69.6 0.2 convolution_add_fusion
  69.9 0.6 constant_dynamic-update-slice_fusion.31
  70.5 0.6 constant_dynamic-update-slice_fusion.30
  71.1 0.6 constant_dynamic-update-slice_fusion.29
  71.7 0.6 constant_dynamic-update-slice_fusion.28
  72.3 0.6 constant_dynamic-update-slice_fusion.27
  73.0 0.6 constant_dynamic-update-slice_fusion.26
  73.6 0.6 constant_dynamic-update-slice_fusion.25
  74.2 0.6 constant_dynamic-update-slice_fusion.24
  74.8 0.6 constant_dynamic-update-slice_fusion.23
  75.4 0.6 constant_dynamic-update-slice_fusion.22
  76.0 0.6 constant_dynamic-update-slice_fusion.21
  76.7 0.6 constant_dynamic-update-slice_fusion.20
  77.3 0.6 constant_dynamic-update-slice_fusion.19
  77.9 0.6 constant_dynamic-update-slice_fusion.18
  78.5 0.6 constant_dynamic-update-slice_fusion.17
  79.1 0.6 constant_dynamic-update-slice_fusion.16
  79.7 3.6 %all-to-all-start.3 = ((f32[16,2,1,16,256]{4,3,1,2,0:T(8,128)}), f32[16,2,1,16,256]{4,3,1,2,0:T(8,128)S(1)}, u32[]{:S(2)}, u32[]{:S(2)}) async-start(f32[16,2,1,16,256]{4,3,1,2,0:T(8,128)} %constant_dynamic-update-slice_fusion.16), calls=%async_computation.3 | async-start | bytes 1048576 | tf_op jit(solution)/shard_map/all_to_all | solution.py:52
  83.3 1.8 %copy.87 = f32[2,128,256]{2,1,0:T(8,128)} copy(f32[2,128,256]{1,2,0:T(8,128)} %get-tuple-element.7) | data formatting | bytes 524288
  85.1 12.4 %all-to-all-done.3 = f32[16,2,1,16,256]{4,3,1,2,0:T(8,128)S(1)} async-done(((f32[16,2,1,16,256]{4,3,1,2,0:T(8,128)}), f32[16,2,1,16,256]{4,3,1,2,0:T(8,128)S(1)}, u32[]{:S(2)}, u32[]{:S(2)}) %all-to-all-start.3) | async-done | bytes 524320 | tf_op jit(solution)/shard_map/all_to_all | solution.py:52
  97.6 0.2 convolution_bitcast_fusion.2
  97.9 0.2 convolution_bitcast_fusion
  98.1 0.3 fusion.5
  98.4 0.2 fusion.7
  98.6 0.4 fusion.21
  99.1 0.3 divide_bitcast_fusion
  99.3 1.5 %broadcast_multiply_fusion = f32[2,512,256]{1,2,0:T(8,128)} fusion(f32[512,256]{0,1:T(8,128)S(1)} %divide_bitcast_fusion, f32[1,512,256]{1,2,0:T(8,128)S(1)} %fusion.7, f32[1,512,256]{1,2,0:T(8,128)S(1)} %fusion.5, f32[512,256]{0,1:T(8,128)S(1)} %divide_bitcast_fusion.1, f32[2,512,256]{1,2,0:T(8,128)S(1)} %copy.63, f32[1,512,256]{1,2,0:T(8,128)S(1)} %fusion.3, ...), kind=kLoop, calls=%fused_computation.113 | loop fusion | flops 2097152 | bytes 5242880 | tf_op jit(solution)/shard_map/mul | solution.py:29
  100.8 2.5 %copy.86 = f32[2,512,256]{2,1,0:T(8,128)} copy(f32[2,512,256]{1,2,0:T(8,128)} %broadcast_multiply_fusion) | data formatting | bytes 2097152
  (38 shorter events, 4.2 us)
Async XLA Ops:
  0.6 1.3 %copy-start.2 = (bf16[2,4,16,512]{3,2,1,0:T(8,128)(2,1)S(1)}, bf16[2,4,16,512]{3,2,1,0:T(8,128)(2,1)}, u32[]{:S(2)}) copy-start(bf16[2,4,16,512]{3,2,1,0:T(8,128)(2,1)} %param.7) | copy-start | bytes 393220
  3.4 7.6 %copy-start.3 = (f32[2,128,256]{2,1,0:T(8,128)S(1)}, f32[2,128,256]{2,1,0:T(8,128)}, u32[]{:S(2)}) copy-start(f32[2,128,256]{2,1,0:T(8,128)} %param.4) | copy-start | bytes 786436
  3.4 17.6 %all-to-all-start = ((bf16[2,16,16,256]{3,2,0,1:T(8,128)(2,1)}), bf16[2,16,16,256]{3,2,0,1:T(8,128)(2,1)S(1)}, u32[]{:S(2)}, u32[]{:S(2)}) async-start(bf16[2,16,16,256]{3,2,0,1:T(8,128)(2,1)} %bitcast.8), calls=%async_computation | async-start | bytes 524288 | tf_op jit(solution)/shard_map/all_to_all | solution.py:43
  11.1 9.9 %copy-start = (bf16[2,128,256]{2,1,0:T(8,128)(2,1)S(1)}, bf16[2,128,256]{2,1,0:T(8,128)(2,1)}, u32[]{:S(2)}) copy-start(bf16[2,128,256]{2,1,0:T(8,128)(2,1)} %param.6) | copy-start | bytes 393220
  31.6 4.8 %copy-start.1 = (f32[2,512,256]{2,1,0:T(8,128)S(1)}, f32[2,512,256]{2,1,0:T(8,128)}, u32[]{:S(2)}) copy-start(f32[2,512,256]{2,1,0:T(8,128)} %param.5) | copy-start | bytes 3145732
  32.8 17.8 %all-to-all-start.1 = ((f32[16,2,1,16,256]{4,3,1,2,0:T(8,128)}), f32[16,2,1,16,256]{4,3,1,2,0:T(8,128)S(1)}, u32[]{:S(2)}, u32[]{:S(2)}) async-start(f32[16,2,1,16,256]{4,3,1,2,0:T(8,128)} %constant_dynamic-update-slice_fusion), calls=%async_computation.1 | async-start | bytes 1048576 | tf_op jit(solution)/shard_map/all_to_all | solution.py:52
  79.7 17.8 %all-to-all-start.3 = ((f32[16,2,1,16,256]{4,3,1,2,0:T(8,128)}), f32[16,2,1,16,256]{4,3,1,2,0:T(8,128)S(1)}, u32[]{:S(2)}, u32[]{:S(2)}) async-start(f32[16,2,1,16,256]{4,3,1,2,0:T(8,128)} %constant_dynamic-update-slice_fusion.16), calls=%async_computation.3 | async-start | bytes 1048576 | tf_op jit(solution)/shard_map/all_to_all | solution.py:52
